TPU v7x, 256 devices: a whole 4x4x8 slice. The times are simulated.
256 devices in a mesh: seq: 32 (over y, z), mp: 8 (over x, core).
Axes of the slice: x: 4, y: 4, z: 8, core: 2. Of those that a mesh axis runs over, the one named last changes fastest.
Arguments:
- out_grad: bfloat16 [16384, 8192], P('seq', 'mp'), may hold values from -6 to 6
- out_weight: bfloat16 [4096, 8192], P('mp'), may hold values from -0.0625 to 0.0625
- queries: bfloat16 [16384, 4096], P('seq', 'mp'), may hold values from -5 to 5
- keys: bfloat16 [64, 128, 4096], P('seq', None, 'mp'), may hold values from -5 to 5
- values: bfloat16 [64, 128, 4096], P('seq', None, 'mp'), may hold values from -6 to 6
- retrieval: int32 [256, 2], replicated, may hold values from 0 to 63, as said below
- counts: int32 [256], P('seq'), may hold values from 1 to 2
Outputs:
- query_grad: bfloat16 [16384, 4096], P('seq', 'mp')
- key_grad: bfloat16 [64, 128, 4096], P('seq', None, 'mp')
- value_grad: bfloat16 [64, 128, 4096], P('seq', None, 'mp')
Inputs may be any that keep to these rules, and one draw needn't show every extreme that they name: `retrieval`: entry e is held by index e // 2 of seq. The 16 neighbour places of one index's blocks name entries of any one owner at most 1 times, and some owner is named exactly 1 times by the blocks of every index.
All inputs are finite; a program needn't handle non-finite values.
Results may differ from a plain program's by a relative error of at most 0.0091.
Values may be sent and summed in bfloat16 or wider, within the bound.
A program may use at most 128 MiB of HBM per device.

v0:
```python
import math
import jax
import jax.numpy as jnp
from jax import lax
from jax.sharding import PartitionSpec as P

HEAD = 128
BLOCK = 64
NEIGH = 2


def rank_slots(owners):
    slot_total = owners.shape[-1]
    earlier_mask = jnp.arange(slot_total)[None, :] < jnp.arange(slot_total)[:, None]
    same_owner = owners[..., :, None] == owners[..., None, :]
    return jnp.sum(same_owner & earlier_mask, axis=-1)


def on_device(out_grad, out_weight, queries, keys, values, retrieval, counts):
    seq_count = lax.axis_size("seq")
    my_index = lax.axis_index("seq")
    tok_rows, head_cols = queries.shape
    entries_here = keys.shape[0]
    nbr_rows = keys.shape[1]
    heads_here = head_cols // HEAD
    blocks_here = tok_rows // BLOCK
    slot_count = blocks_here * NEIGH
    slot_cap = (slot_count + seq_count - 1) // seq_count
    score_scale = 1.0 / math.sqrt(HEAD)
    grad_out = lax.dot_general(
        lax.all_gather(out_grad, "mp", axis=1, tiled=True),
        out_weight,
        (((1,), (1,)), ((), ())),
        preferred_element_type=jnp.float32,
    ).astype(jnp.bfloat16)
    all_lists = retrieval.reshape(seq_count, slot_count)
    owners = all_lists // entries_here
    all_ranks = rank_slots(owners)
    my_lists = lax.dynamic_index_in_dim(all_lists, my_index, 0, keepdims=False)
    my_owner = my_lists // entries_here
    my_rank = lax.dynamic_index_in_dim(all_ranks, my_index, 0, keepdims=False)
    flat_slot = my_owner * slot_cap + my_rank
    chosen = (owners == my_index)[:, None, :] & (
        all_ranks[:, None, :] == jnp.arange(slot_cap)[None, :, None]
    )
    filled = jnp.any(chosen, axis=2)
    picked = jnp.sum(jnp.where(chosen, all_lists[:, None, :] % entries_here, 0), axis=2)
    all_keys, all_values = (
        lax.all_gather(keys, "seq", axis=0, tiled=True),
        lax.all_gather(values, "seq", axis=0, tiled=True),
    )
    slot_keys = jnp.take(all_keys, my_lists, axis=0)
    slot_values = jnp.take(all_values, my_lists, axis=0)
    query_rows = queries.reshape(blocks_here, BLOCK, heads_here, HEAD)
    grad_rows = grad_out.reshape(blocks_here, BLOCK, heads_here, HEAD)
    key_rows = slot_keys.reshape(blocks_here, NEIGH * nbr_rows, heads_here, HEAD)
    value_rows = slot_values.reshape(blocks_here, NEIGH * nbr_rows, heads_here, HEAD)
    live_keys = jnp.arange(NEIGH * nbr_rows)[None, :] < (counts * nbr_rows)[:, None]
    live_mask = live_keys[:, None, None, :]
    scores = (
        jnp.einsum("cqhe,ckhe->chqk", query_rows, key_rows, preferred_element_type=jnp.float32)
        * score_scale
    )
    row_max = jnp.max(jnp.where(live_mask, scores, -jnp.inf), axis=-1, keepdims=True)
    raised = jnp.where(live_mask, jnp.exp(scores - row_max), 0.0)
    attn_weights = raised / jnp.sum(raised, axis=-1, keepdims=True)
    weights_low = attn_weights.astype(jnp.bfloat16)
    attn_out = jnp.einsum(
        "chqk,ckhe->cqhe", weights_low, value_rows, preferred_element_type=jnp.float32
    )
    row_dot = jnp.sum(grad_rows.astype(jnp.float32) * attn_out, axis=-1)
    grad_weights = jnp.einsum(
        "cqhe,ckhe->chqk", grad_rows, value_rows, preferred_element_type=jnp.float32
    )
    grad_scores = attn_weights * (grad_weights - jnp.transpose(row_dot, (0, 2, 1))[..., None])
    grad_low = grad_scores.astype(jnp.bfloat16)
    query_grad = (
        (
            jnp.einsum("chqk,ckhe->cqhe", grad_low, key_rows, preferred_element_type=jnp.float32)
            * score_scale
        )
        .astype(jnp.bfloat16)
        .reshape(tok_rows, head_cols)
    )
    key_terms = (
        (
            jnp.einsum("chqk,cqhe->ckhe", grad_low, query_rows, preferred_element_type=jnp.float32)
            * score_scale
        )
        .astype(jnp.bfloat16)
        .reshape(slot_count, nbr_rows, head_cols)
    )
    value_terms = (
        jnp.einsum("chqk,cqhe->ckhe", weights_low, grad_rows, preferred_element_type=jnp.float32)
        .astype(jnp.bfloat16)
        .reshape(slot_count, nbr_rows, head_cols)
    )
    key_back = (
        jnp.zeros((seq_count * slot_cap, nbr_rows, head_cols), jnp.bfloat16)
        .at[flat_slot]
        .set(key_terms)
        .reshape(seq_count, slot_cap, nbr_rows, head_cols)
    )
    value_back = (
        jnp.zeros((seq_count * slot_cap, nbr_rows, head_cols), jnp.bfloat16)
        .at[flat_slot]
        .set(value_terms)
        .reshape(seq_count, slot_cap, nbr_rows, head_cols)
    )
    back_keys, back_values = (
        lax.all_to_all(key_back, "seq", split_axis=0, concat_axis=0, tiled=True),
        lax.all_to_all(value_back, "seq", split_axis=0, concat_axis=0, tiled=True),
    )
    summing = (
        ((picked[None, :, :] == jnp.arange(entries_here)[:, None, None]) & filled[None, :, :])
        .astype(jnp.bfloat16)
        .reshape(entries_here, seq_count * slot_cap)
    )
    key_grad = (
        jnp.dot(
            summing,
            back_keys.reshape(seq_count * slot_cap, nbr_rows * head_cols),
            preferred_element_type=jnp.float32,
        )
        .astype(jnp.bfloat16)
        .reshape(entries_here, nbr_rows, head_cols)
    )
    value_grad = (
        jnp.dot(
            summing,
            back_values.reshape(seq_count * slot_cap, nbr_rows * head_cols),
            preferred_element_type=jnp.float32,
        )
        .astype(jnp.bfloat16)
        .reshape(entries_here, nbr_rows, head_cols)
    )
    return (query_grad, key_grad, value_grad)


def solution(mesh):
    return jax.shard_map(
        on_device,
        mesh=mesh,
        in_specs=(
            P("seq", "mp"),
            P("mp", None),
            P("seq", "mp"),
            P("seq", None, "mp"),
            P("seq", None, "mp"),
            P(),
            P("seq"),
        ),
        out_specs=(P("seq", "mp"), P("seq", None, "mp"), P("seq", None, "mp")),
        check_vma=False,
    )
```

profile of v0, /device:TPU:2, one launch (start us, length us, event | category | flops | bytes accessed | tf_op | source)
XLA Modules:
  0.0 513.0 jit_solution(1532240102834940952)
XLA Ops:
  7.2 0.0 copy-start.6
  7.2 0.0 copy-start.7
  7.2 0.0 all-gather.6.cloned.1.call-start
  7.2 0.7 all-gather.6.cloned.1.call-update
  7.9 0.0 all-gather.4.cloned.1.call-start
  8.0 0.7 all-gather.4.cloned.1.call-update
  8.7 0.0 all-gather.8.cloned.1.call-start
  8.7 0.7 all-gather.8.cloned.1.call-update
  9.4 0.8 copy.93
  10.2 0.1 reshape.442
  10.3 0.0 copy-done.6
  10.3 0.1 reshape.444
  10.5 0.1 copy.107
  10.6 0.1 convert_reduce_fusion
  10.7 0.2 dynamic-slice_reduce_fusion
  10.9 0.0 copy-done.7
  11.0 0.1 iota_compare_fusion.1
  11.0 53.3 %all-gather.6.cloned.1.call-done = bf16[512,8192]{1,0:T(8,128)(2,1)} async-done(((bf16[512,1024]{1,0:T(8,128)(2,1)}), bf16[512,8192]{1,0:T(8,128)(2,1)}) %all-gather.6.cloned.1.call-update) | async-done | bytes 8388624 | tf_op jit(solution)/shard_map/all_gather | solution.py:31
  64.3 10.3 %convolution_convert_fusion.2 = bf16[512,512]{1,0:T(8,128)(2,1)S(1)} fusion(bf16[512,8192]{1,0:T(8,128)(2,1)} %all-gather.6.cloned.1.call-done, bf16[512,8192]{1,0:T(8,128)(2,1)} %param.10), kind=kOutput, calls=%fused_computation.31 | convolution fusion | flops 4295229440 | bytes 17301504 | tf_op jit(solution)/shard_map/dot_general | solution.py:30
  74.6 0.1 reshape.445
  74.7 91.7 %all-gather.4.cloned.1.call-done = bf16[64,128,512]{2,1,0:T(8,128)(2,1)} async-done(((bf16[2,128,512]{2,1,0:T(8,128)(2,1)}), bf16[64,128,512]{2,1,0:T(8,128)(2,1)}) %all-gather.4.cloned.1.call-update) | async-done | bytes 8388624 | tf_op jit(solution)/shard_map/all_gather | solution.py:49
  166.4 4.1 gather_fusion
  170.5 94.1 %all-gather.8.cloned.1.call-done = bf16[64,128,512]{2,1,0:T(8,128)(2,1)} async-done(((bf16[2,128,512]{2,1,0:T(8,128)(2,1)}), bf16[64,128,512]{2,1,0:T(8,128)(2,1)}) %all-gather.8.cloned.1.call-update) | async-done | bytes 8388624 | tf_op jit(solution)/shard_map/all_gather | solution.py:50
  264.7 5.4 %gather_fusion.1 = bf16[16,128,512]{2,1,0:T(8,128)(2,1)} fusion(bf16[64,128,512]{2,1,0:T(8,128)(2,1)} %all-gather.8.cloned.1.call-done, s32[1024]{0:T(1024)S(1)} %pad_clamp_fusion), kind=kCustom, calls=%fused_computation.1.clone | custom fusion | bytes 4194368 | tf_op jit(solution)/shard_map/jit(_take)/gather | solution.py:53
  270.1 4.0 broadcast_select_fusion.1
  274.0 2.5 reshape.443
  276.6 0.0 copy-start.1
  276.6 0.8 fusion.5
  277.4 0.5 copy-done.1
  277.9 1.7 bitcast_reduce_fusion
  279.7 0.0 copy-start.8
  279.7 1.3 copy-done.8
  281.0 0.9 convert_bitcast_fusion
  281.9 2.5 copy.120
  284.4 2.7 reshape.496
  287.1 2.4 broadcast.352.clone
  289.6 5.2 %scatter_fusion.1 = bf16[32,128,512]{2,1,0:T(8,128)(2,1)} fusion(bf16[32,128,512]{2,1,0:T(8,128)(2,1)} %broadcast.352.clone, s32[16]{0:T(128)S(1)} %fusion.53, bf16[16,128,512]{2,1,0:T(8,128)(2,1)S(1)} %reshape.496), kind=kCustom, calls=%fused_computation.3 | custom fusion | bytes 6291520 | tf_op jit(solution)/shard_map/scatter | solution.py:107
  294.8 6.1 %all-to-all-start.1 = ((bf16[32,1,128,512]{3,2,1,0:T(8,128)(2,1)}), bf16[32,1,128,512]{3,2,1,0:T(8,128)(2,1)}, u32[]{:S(2)}, u32[]{:S(2)}) async-start(bf16[32,1,128,512]{3,2,1,0:T(8,128)(2,1)} %bitcast.79), calls=%async_computation.1 | async-start | bytes 8388608 | tf_op jit(solution)/shard_map/all_to_all | solution.py:112
  300.9 0.0 copy-done.3
  300.9 2.1 reshape.446
  302.9 3.1 fusion.28
  306.0 0.0 copy-done.4
  306.0 0.4 copy-done.9
  306.4 1.0 multiply_convert_fusion.1
  307.5 0.0 copy-start.5
  307.5 0.8 fusion.13
  308.3 0.1 copy-done.5
  308.4 2.9 copy.119
  311.4 2.7 reshape.495
  314.1 2.4 broadcast.352.clone.1
  316.5 5.2 %scatter_fusion = bf16[32,128,512]{2,1,0:T(8,128)(2,1)} fusion(bf16[32,128,512]{2,1,0:T(8,128)(2,1)} %broadcast.352.clone.1, s32[16]{0:T(128)S(1)} %fusion.53, bf16[16,128,512]{2,1,0:T(8,128)(2,1)S(1)} %reshape.495), kind=kCustom, calls=%fused_computation.2 | custom fusion | bytes 6291520 | tf_op jit(solution)/shard_map/scatter | solution.py:101
  321.8 75.5 %all-to-all-done.1 = bf16[32,1,128,512]{3,2,1,0:T(8,128)(2,1)} async-done(((bf16[32,1,128,512]{3,2,1,0:T(8,128)(2,1)}), bf16[32,1,128,512]{3,2,1,0:T(8,128)(2,1)}, u32[]{:S(2)}, u32[]{:S(2)}) %all-to-all-start.1) | async-done | bytes 4194336 | tf_op jit(solution)/shard_map/all_to_all | solution.py:112
  397.3 5.5 %all-to-all-start = ((bf16[32,1,128,512]{3,2,1,0:T(8,128)(2,1)}), bf16[32,1,128,512]{3,2,1,0:T(8,128)(2,1)}, u32[]{:S(2)}, u32[]{:S(2)}) async-start(bf16[32,1,128,512]{3,2,1,0:T(8,128)(2,1)} %bitcast.78), calls=%async_computation | async-start | bytes 8388608 | tf_op jit(solution)/shard_map/all_to_all | solution.py:111
  402.8 0.1 reshape.448
  402.9 0.1 copy.103
  403.1 1.7 fusion.31
  404.7 0.4 copy.101
  405.2 0.9 copy.162
  406.0 6.5 %copy.126 = bf16[4,8,128,512]{3,1,2,0:T(8,128)(2,1)} copy(bf16[4,8,128,512]{3,2,1,0:T(8,128)(2,1)} %bitcast.27) | data formatting | bytes 8388608
  412.5 87.0 %all-to-all-done = bf16[32,1,128,512]{3,2,1,0:T(8,128)(2,1)} async-done(((bf16[32,1,128,512]{3,2,1,0:T(8,128)(2,1)}), bf16[32,1,128,512]{3,2,1,0:T(8,128)(2,1)}, u32[]{:S(2)}, u32[]{:S(2)}) %all-to-all-start) | async-done | bytes 4194336 | tf_op jit(solution)/shard_map/all_to_all | solution.py:111
  499.6 4.7 copy.124
  504.3 0.7 convolution_convert_fusion
  504.9 0.7 convolution_convert_fusion.1
  505.6 0.8 copy_bitcast_fusion.1
  (15 shorter events, 0.1 us)
Async XLA Ops:
  7.2 3.2 copy-start.6
  7.2 3.7 copy-start.7
  7.2 57.1 %all-gather.6.cloned.1.call-start = ((), (), s32[]{:S(2)}) async-start(), calls=%async_computation.3 | async-start | bytes 9437184 | tf_op jit(solution)/shard_map/all_gather | solution.py:31
  7.9 158.5 %all-gather.4.cloned.1.call-start = ((), (), s32[]{:S(2)}) async-start(), calls=%async_computation.2 | async-start | bytes 8650752 | tf_op jit(solution)/shard_map/all_gather | solution.py:49
  8.7 256.0 %all-gather.8.cloned.1.call-start = ((), (), s32[]{:S(2)}) async-start(), calls=%async_computation.4 | async-start | bytes 8650752 | tf_op jit(solution)/shard_map/all_gather | solution.py:50
  276.6 1.4 copy-start.1
  279.7 1.3 copy-start.8
  294.8 6.1 %copy-start.3 = (bf16[16,128,512]{2,1,0:T(8,128)(2,1)S(1)}, bf16[16,128,512]{2,1,0:T(8,128)(2,1)}, u32[]{:S(2)}) copy-start(bf16[16,128,512]{2,1,0:T(8,128)(2,1)} %get-tuple-element.9) | copy-start | bytes 6291460
  294.8 102.5 %all-to-all-start.1 = ((bf16[32,1,128,512]{3,2,1,0:T(8,128)(2,1)}), bf16[32,1,128,512]{3,2,1,0:T(8,128)(2,1)}, u32[]{:S(2)}, u32[]{:S(2)}) async-start(bf16[32,1,128,512]{3,2,1,0:T(8,128)(2,1)} %bitcast.79), calls=%async_computation.1 | async-start | bytes 8388608 | tf_op jit(solution)/shard_map/all_to_all | solution.py:112
  302.9 3.1 copy-start.4
  302.9 3.5 copy-start.9
  307.5 1.0 copy-start.5
  397.3 5.8 %copy-start.2 = (bf16[8,256,4,128]{3,2,1,0:T(4,128)(2,1)S(1)}, bf16[8,256,4,128]{3,2,1,0:T(4,128)(2,1)}, u32[]{:S(2)}) copy-start(bf16[8,256,4,128]{3,2,1,0:T(4,128)(2,1)} %copy-done.1) | copy-start | bytes 6291460
  397.3 102.3 %all-to-all-start = ((bf16[32,1,128,512]{3,2,1,0:T(8,128)(2,1)}), bf16[32,1,128,512]{3,2,1,0:T(8,128)(2,1)}, u32[]{:S(2)}, u32[]{:S(2)}) async-start(bf16[32,1,128,512]{3,2,1,0:T(8,128)(2,1)} %bitcast.78), calls=%async_computation | async-start | bytes 8388608 | tf_op jit(solution)/shard_map/all_to_all | solution.py:111
  499.6 4.7 copy-start
Sparse Core Ops, SparseCore 0:
  9.9 54.4 all-gather.5
  66.9 99.4 all-gather.3
  169.0 95.5 all-gather.7
where the time goes:
time: 514 us; the launch traced here: 513 us
  waiting for transfers between devices  404 us (79%)
  local copies, waits for them, and re-layouts  57.5 us (11%)
  matrix products  20 us (4%)
  between operations  14 us (3%)
  starting transfers between devices  11.7 us (2%)
  other arithmetic  5.99 us (1%)
    all_gather x1, waiting for transfers between devices, on_device(): lax.all_gather(values, 'seq', axis=0, tiled=True)  94.1 us
    all_gather x1, waiting for transfers between devices, on_device(): lax.all_gather(keys, 'seq', axis=0, tiled=True)  91.7 us
    all_to_all x1, waiting for transfers between devices, on_device(): lax.all_to_all(key_back, 'seq', split_axis=0, concat_axis=0, tiled=True)  87 us
    all_to_all x1, waiting for transfers between devices, on_device(): lax.all_to_all(value_back, 'seq', split_axis=0, concat_axis=0, tiled=True)  75.5 us
    all_gather x1, waiting for transfers between devices, on_device(): lax.all_gather(out_grad, 'mp', axis=1, tiled=True)  53.3 us
    unnamed x24, local copies, waits for them, and re-layouts  15.3 us
    dot_general x1, matrix products, on_device(): lax.dot_general(lax.all_gather(out_grad, 'mp', axis=1, tiled=True), out_w...  10.3 us
  transfers between devices with their start and end apart: 5, of which 5 were waited for; matrix products, arithmetic and copies ran while one was open for 9% of the time, Pallas kernels for 0%

commit v1 on v0

--- a/solution.py
+++ b/solution.py
@@ -7,6 +7,28 @@
 HEAD = 128
 BLOCK = 64
 NEIGH = 2
+
+
+def in_order(pieces, dim):
+    pieces = jnp.moveaxis(pieces, 0, dim)
+    lengths = pieces.shape
+    return pieces.reshape(*lengths[:dim], lengths[dim] * lengths[dim + 1], *lengths[dim + 2 :])
+
+
+def collect(value, axis, dim):
+    size = lax.axis_size(axis)
+    pairs = [(i, (i + 1) % size) for i in range(size)]
+    back = [(b, a) for a, b in pairs]
+    lower, upper = ([], [])
+    for lap in range(size - 1):
+        if lap % 2 == 0:
+            lower.append(lax.ppermute(lower[-1] if lower else value, axis, pairs))
+        else:
+            upper.append(lax.ppermute(upper[-1] if upper else value, axis, back))
+    blocks = jnp.stack([*lower[::-1], value, *upper])
+    shift = lax.axis_index(axis) - len(lower)
+    blocks = blocks[(jnp.arange(size) - shift) % size]
+    return in_order(blocks, dim)
 
 
 def rank_slots(owners):
@@ -28,7 +50,7 @@
     slot_cap = (slot_count + seq_count - 1) // seq_count
     score_scale = 1.0 / math.sqrt(HEAD)
     grad_out = lax.dot_general(
-        lax.all_gather(out_grad, "mp", axis=1, tiled=True),
+        collect(out_grad, "mp", 1),
         out_weight,
         (((1,), (1,)), ((), ())),
         preferred_element_type=jnp.float32,

time: 514 us -> 460 us (0.89)
  waiting for transfers between devices: 404 us -> 309 us
  local copies, waits for them, and re-layouts: 57.5 us -> 92.1 us
  starting transfers between devices: 11.7 us -> 16.9 us
    all_gather x1, waiting for transfers between devices: 91.7 us -> 1.48 us  [on_device(): lax.all_gather(keys, 'seq', axis=0, tiled=True)]
    all_gather x1 -> x0, waiting for transfers between devices: 53.3 us -> none  [on_device(): lax.all_gather(out_grad, 'mp', axis=1, tiled=True)]
    ppermute x0 -> x7, waiting for transfers between devices: none -> 49.3 us  [the longest x4 49.3 us: collect(): lower.append(lax.ppermute(lower[-1] if lower else value, axis, pairs))]
    unnamed x24 -> x29, local copies, waits for them, and re-layouts: 15.3 us -> 27.8 us
    transpose x0 -> x1, local copies, waits for them, and re-layouts: none -> 11.5 us  [in_order(): pieces = jnp.moveaxis(pieces, 0, dim)]
    gather x0 -> x1, local copies, waits for them, and re-layouts: none -> 8.19 us  [collect(): blocks = blocks[(jnp.arange(size) - shift) % size]]
    ppermute x0 -> x7, starting transfers between devices: none -> 5.26 us  [the longest x3 5.24 us: collect(): upper.append(lax.ppermute(upper[-1] if upper else value, axis, back))]
  transfers between devices with their start and end apart: 5 -> 11, of which waited for: 5 -> 8; matrix products, arithmetic and copies ran while one was open for 9% -> 18% of each run, Pallas kernels for 0% -> 0%
where the time goes in v1:
time: 460 us; the launch traced here: 459 us
  waiting for transfers between devices  309 us (67%)
  local copies, waits for them, and re-layouts  92.1 us (20%)
  matrix products  20.2 us (4%)
  starting transfers between devices  16.9 us (4%)
  between operations  14.3 us (3%)
  other arithmetic  6.68 us (1%)
    all_gather x1, waiting for transfers between devices, on_device(): lax.all_gather(values, 'seq', axis=0, tiled=True)  94.1 us
    all_to_all x1, waiting for transfers between devices, on_device(): lax.all_to_all(key_back, 'seq', split_axis=0, concat_axis=0, tiled=True)  86.9 us
    all_to_all x1, waiting for transfers between devices, on_device(): lax.all_to_all(value_back, 'seq', split_axis=0, concat_axis=0, tiled=True)  75.4 us
    ppermute x4, waiting for transfers between devices, collect(): lower.append(lax.ppermute(lower[-1] if lower else value, axis, pairs))  49.3 us
    unnamed x29, local copies, waits for them, and re-layouts  27.8 us
    transpose x1, local copies, waits for them, and re-layouts, in_order(): pieces = jnp.moveaxis(pieces, 0, dim)  11.5 us
    dot_general x1, matrix products, on_device(): lax.dot_general(collect(out_grad, 'mp', 1), out_weight, (((1,), (1,)), ((...  10.5 us
  transfers between devices with their start and end apart: 11, of which 8 were waited for; matrix products, arithmetic and copies ran while one was open for 18% of the time, Pallas kernels for 0%

profile of v1, /device:TPU:2, one launch (start us, length us, event | category | flops | bytes accessed | tf_op | source)
XLA Modules:
  0.0 458.8 jit_solution(9793011754535120685)
XLA Ops:
  7.2 0.7 all-gather.3.cloned.1.call-update
  7.9 0.7 all-gather.5.cloned.1.call-update
  8.7 14.4 %collective-permute-done = bf16[512,1024]{1,0:T(8,128)(2,1)S(1)} collective-permute-done((bf16[512,1024]{1,0:T(8,128)(2,1)}, bf16[512,1024]{1,0:T(8,128)(2,1)S(1)}, u32[]{:S(2)}, u32[]{:S(2)}) %collective-permute-start) | collective-permute-done | bytes 1048608 | tf_op jit(solution)/shard_map/ppermute | solution.py:25
  23.1 1.7 collective-permute-start.4
  24.8 12.6 %collective-permute-done.1 = bf16[512,1024]{1,0:T(8,128)(2,1)} collective-permute-done((bf16[512,1024]{1,0:T(8,128)(2,1)S(1)}, bf16[512,1024]{1,0:T(8,128)(2,1)}, u32[]{:S(2)}, u32[]{:S(2)}) %collective-permute-start.1) | collective-permute-done | bytes 1048608 | tf_op jit(solution)/shard_map/ppermute | solution.py:25
  37.4 0.8 copy.96
  38.2 0.1 reshape.494
  38.4 0.1 convert_reduce_fusion
  38.6 1.8 collective-permute-start.5
  40.3 11.6 %collective-permute-done.2 = bf16[512,1024]{1,0:T(8,128)(2,1)} collective-permute-done((bf16[512,1024]{1,0:T(8,128)(2,1)}, bf16[512,1024]{1,0:T(8,128)(2,1)}, u32[]{:S(2)}, u32[]{:S(2)}) %collective-permute-start.2) | collective-permute-done | bytes 1048608 | tf_op jit(solution)/shard_map/ppermute | solution.py:25
  52.0 1.2 reshape.496
  53.2 0.2 dynamic-slice_reduce_fusion
  53.4 0.7 broadcast_multiply_fusion
  54.1 1.7 collective-permute-start.6
  55.9 10.6 %collective-permute-done.3 = bf16[512,1024]{1,0:T(8,128)(2,1)} collective-permute-done((bf16[512,1024]{1,0:T(8,128)(2,1)}, bf16[512,1024]{1,0:T(8,128)(2,1)}, u32[]{:S(2)}, u32[]{:S(2)}) %collective-permute-start.3) | collective-permute-done | bytes 1048608 | tf_op jit(solution)/shard_map/ppermute | solution.py:25
  66.5 2.3 bitcast_dynamic-update-slice_fusion.7
  68.8 2.3 bitcast_dynamic-update-slice_fusion.6
  71.1 2.4 bitcast_dynamic-update-slice_fusion.5
  73.5 1.1 bitcast_dynamic-update-slice_fusion.4
  74.6 1.0 bitcast_dynamic-update-slice_fusion.3
  75.6 1.1 bitcast_dynamic-update-slice_fusion.2
  76.7 2.3 bitcast_dynamic-update-slice_fusion.1
  79.0 1.1 bitcast_dynamic-update-slice_fusion
  80.1 8.2 %gather_fusion = bf16[8,512,1024]{2,1,0:T(8,128)(2,1)} fusion(bf16[8,512,1024]{2,1,0:T(8,128)(2,1)} %bitcast_dynamic-update-slice_fusion, s32[1024]{0:T(1024)S(1)} %pad_clamp_fusion), kind=kCustom, calls=%fused_computation.2 | custom fusion | bytes 16777248 | tf_op jit(solution)/shard_map/gather | solution.py:30
  88.3 11.5 %copy.99 = bf16[512,8,1024]{0,2,1:T(8,128)(2,1)} copy(bf16[512,8,1024]{2,0,1:T(8,128)(2,1)} %bitcast.98) | data formatting | bytes 16777216 | tf_op jit(solution)/shard_map/transpose | solution.py:13
  99.8 10.5 %convolution_convert_fusion.2 = bf16[512,512]{1,0:T(8,128)(2,1)S(1)} fusion(bf16[512,8192]{0,1:T(8,128)(2,1)} %bitcast.103, bf16[512,8192]{1,0:T(8,128)(2,1)} %param.10), kind=kOutput, calls=%fused_computation.31 | convolution fusion | flops 4295229440 | bytes 17301504 | tf_op jit(solution)/shard_map/dot_general | solution.py:52
  110.3 0.1 reshape.498
  110.4 1.5 all-gather.3.cloned.1.call-done
  111.9 4.1 gather_fusion.1
  116.0 94.1 %all-gather.5.cloned.1.call-done = bf16[64,128,512]{2,1,0:T(8,128)(2,1)} async-done(((bf16[2,128,512]{2,1,0:T(8,128)(2,1)}), bf16[64,128,512]{2,1,0:T(8,128)(2,1)}) %all-gather.5.cloned.1.call-update) | async-done | bytes 8388624 | tf_op jit(solution)/shard_map/all_gather | solution.py:72
  210.1 5.4 %gather_fusion.2 = bf16[16,128,512]{2,1,0:T(8,128)(2,1)} fusion(bf16[64,128,512]{2,1,0:T(8,128)(2,1)} %all-gather.5.cloned.1.call-done, s32[1024]{0:T(1024)S(1)} %pad_clamp_fusion.1), kind=kCustom, calls=%fused_computation.1.clone | custom fusion | bytes 4194368 | tf_op jit(solution)/shard_map/jit(_take)/gather | solution.py:75
  215.5 4.0 broadcast_select_fusion.1
  219.5 2.5 reshape.495
  222.1 0.8 fusion.5
  222.9 0.5 copy-done.1
  223.4 1.7 bitcast_reduce_fusion
  225.2 1.3 copy-done.7
  226.5 0.9 convert_bitcast_fusion
  227.4 2.5 copy.124
  229.9 2.7 reshape.557
  232.7 2.4 broadcast.416.clone
  235.1 5.3 %scatter_fusion.1 = bf16[32,128,512]{2,1,0:T(8,128)(2,1)} fusion(bf16[32,128,512]{2,1,0:T(8,128)(2,1)} %broadcast.416.clone, s32[16]{0:T(128)S(1)} %fusion.55, bf16[16,128,512]{2,1,0:T(8,128)(2,1)S(1)} %reshape.557), kind=kCustom, calls=%fused_computation.4 | custom fusion | bytes 6291520 | tf_op jit(solution)/shard_map/scatter | solution.py:129
  240.4 6.0 %all-to-all-start.1 = ((bf16[32,1,128,512]{3,2,1,0:T(8,128)(2,1)}), bf16[32,1,128,512]{3,2,1,0:T(8,128)(2,1)}, u32[]{:S(2)}, u32[]{:S(2)}) async-start(bf16[32,1,128,512]{3,2,1,0:T(8,128)(2,1)} %bitcast.100), calls=%async_computation.1 | async-start | bytes 8388608 | tf_op jit(solution)/shard_map/all_to_all | solution.py:134
  246.4 2.1 reshape.499
  248.5 3.1 fusion.28
  251.6 0.4 copy-done.8
  252.0 1.0 multiply_convert_fusion.1
  253.1 0.8 fusion.13
  253.9 0.1 copy-done.5
  254.0 3.0 copy.123
  257.0 2.7 reshape.556
  259.7 2.4 broadcast.416.clone.1
  262.2 5.2 %scatter_fusion = bf16[32,128,512]{2,1,0:T(8,128)(2,1)} fusion(bf16[32,128,512]{2,1,0:T(8,128)(2,1)} %broadcast.416.clone.1, s32[16]{0:T(128)S(1)} %fusion.55, bf16[16,128,512]{2,1,0:T(8,128)(2,1)S(1)} %reshape.556), kind=kCustom, calls=%fused_computation.3 | custom fusion | bytes 6291520 | tf_op jit(solution)/shard_map/scatter | solution.py:123
  267.4 75.4 %all-to-all-done.1 = bf16[32,1,128,512]{3,2,1,0:T(8,128)(2,1)} async-done(((bf16[32,1,128,512]{3,2,1,0:T(8,128)(2,1)}), bf16[32,1,128,512]{3,2,1,0:T(8,128)(2,1)}, u32[]{:S(2)}, u32[]{:S(2)}) %all-to-all-start.1) | async-done | bytes 4194336 | tf_op jit(solution)/shard_map/all_to_all | solution.py:134
  342.8 5.5 %all-to-all-start = ((bf16[32,1,128,512]{3,2,1,0:T(8,128)(2,1)}), bf16[32,1,128,512]{3,2,1,0:T(8,128)(2,1)}, u32[]{:S(2)}, u32[]{:S(2)}) async-start(bf16[32,1,128,512]{3,2,1,0:T(8,128)(2,1)} %bitcast.99), calls=%async_computation | async-start | bytes 8388608 | tf_op jit(solution)/shard_map/all_to_all | solution.py:133
  348.6 1.7 fusion.31
  350.3 0.4 copy.105
  350.7 0.9 copy.166
  351.6 6.5 %copy.130 = bf16[4,8,128,512]{3,1,2,0:T(8,128)(2,1)} copy(bf16[4,8,128,512]{3,2,1,0:T(8,128)(2,1)} %bitcast.38) | data formatting | bytes 8388608
  358.1 86.9 %all-to-all-done = bf16[32,1,128,512]{3,2,1,0:T(8,128)(2,1)} async-done(((bf16[32,1,128,512]{3,2,1,0:T(8,128)(2,1)}), bf16[32,1,128,512]{3,2,1,0:T(8,128)(2,1)}, u32[]{:S(2)}, u32[]{:S(2)}) %all-to-all-start) | async-done | bytes 4194336 | tf_op jit(solution)/shard_map/all_to_all | solution.py:133
  445.0 4.7 %copy.128 = bf16[4,8,128,512]{3,1,2,0:T(8,128)(2,1)S(1)} copy(bf16[4,8,128,512]{3,2,1,0:T(8,128)(2,1)} %bitcast.33) | data formatting | bytes 8388608
  449.8 0.7 convolution_convert_fusion
  450.4 0.7 convolution_convert_fusion.1
  451.1 0.8 copy_bitcast_fusion.1
  (36 shorter events, 0.6 us)
Async XLA Ops:
  7.2 104.8 %all-gather.3.cloned.1.call-start = ((), (), s32[]{:S(2)}) async-start(), calls=%async_computation.2 | async-start | bytes 8650752 | tf_op jit(solution)/shard_map/all_gather | solution.py:71
  7.9 202.2 %all-gather.5.cloned.1.call-start = ((), (), s32[]{:S(2)}) async-start(), calls=%async_computation.3 | async-start | bytes 8650752 | tf_op jit(solution)/shard_map/all_gather | solution.py:72
  8.6 14.4 %collective-permute-start = (bf16[512,1024]{1,0:T(8,128)(2,1)}, bf16[512,1024]{1,0:T(8,128)(2,1)S(1)}, u32[]{:S(2)}, u32[]{:S(2)}) collective-permute-start(bf16[512,1024]{1,0:T(8,128)(2,1)} %param.9), channel_id=1, source_target_pairs={{0,1},{1,2},{2,3},{3,4},{4,5},{5,6},{6,7},{7,0},{8,9},{9,10},{10,1... | collective-permute-start | bytes 3145736 | tf_op jit(solution)/shard_map/ppermute | solution.py:25
  23.1 14.3 %collective-permute-start.1 = (bf16[512,1024]{1,0:T(8,128)(2,1)S(1)}, bf16[512,1024]{1,0:T(8,128)(2,1)}, u32[]{:S(2)}, u32[]{:S(2)}) collective-permute-start(bf16[512,1024]{1,0:T(8,128)(2,1)S(1)} %collective-permute-done), channel_id=1, source_target_pairs={{0,1},{1,2},{2,3},{3,4},{4,5},{5,6},{6,7},{7,0},{8,9},{9,10},{10,1... | collective-permute-start | bytes 3145736 | tf_op jit(solution)/shard_map/ppermute | solution.py:25
  23.1 15.5 %collective-permute-start.4 = (bf16[512,1024]{1,0:T(8,128)(2,1)}, bf16[512,1024]{1,0:T(8,128)(2,1)S(1)}, u32[]{:S(2)}, u32[]{:S(2)}) collective-permute-start(bf16[512,1024]{1,0:T(8,128)(2,1)} %param.9), channel_id=1, source_target_pairs={{1,0},{2,1},{3,2},{4,3},{5,4},{6,5},{7,6},{0,7},{9,8},{10,9},{11,1... | collective-permute-start | bytes 3145736 | tf_op jit(solution)/shard_map/ppermute | solution.py:27
  37.4 14.5 %collective-permute-start.2 = (bf16[512,1024]{1,0:T(8,128)(2,1)}, bf16[512,1024]{1,0:T(8,128)(2,1)}, u32[]{:S(2)}, u32[]{:S(2)}) collective-permute-start(bf16[512,1024]{1,0:T(8,128)(2,1)} %collective-permute-done.1), channel_id=1, source_target_pairs={{0,1},{1,2},{2,3},{3,4},{4,5},{5,6},{6,7},{7,0},{8,9},{9,10},{10,1... | collective-permute-start | bytes 3145736 | tf_op jit(solution)/shard_map/ppermute | solution.py:25
  38.6 15.6 %collective-permute-start.5 = (bf16[512,1024]{1,0:T(8,128)(2,1)S(1)}, bf16[512,1024]{1,0:T(8,128)(2,1)}, u32[]{:S(2)}, u32[]{:S(2)}) collective-permute-start(bf16[512,1024]{1,0:T(8,128)(2,1)S(1)} %collective-permute-done.4), channel_id=1, source_target_pairs={{1,0},{2,1},{3,2},{4,3},{5,4},{6,5},{7,6},{0,7},{9,8},{10,9},{11,1... | collective-permute-start | bytes 3145736 | tf_op jit(solution)/shard_map/ppermute | solution.py:27
  52.0 14.5 %collective-permute-start.3 = (bf16[512,1024]{1,0:T(8,128)(2,1)}, bf16[512,1024]{1,0:T(8,128)(2,1)}, u32[]{:S(2)}, u32[]{:S(2)}) collective-permute-start(bf16[512,1024]{1,0:T(8,128)(2,1)} %collective-permute-done.2), channel_id=1, source_target_pairs={{0,1},{1,2},{2,3},{3,4},{4,5},{5,6},{6,7},{7,0},{8,9},{9,10},{10,1... | collective-permute-start | bytes 3145736 | tf_op jit(solution)/shard_map/ppermute | solution.py:25
  54.1 24.9 %collective-permute-start.6 = (bf16[512,1024]{1,0:T(8,128)(2,1)}, bf16[512,1024]{1,0:T(8,128)(2,1)S(1)}, u32[]{:S(2)}, u32[]{:S(2)}) collective-permute-start(bf16[512,1024]{1,0:T(8,128)(2,1)} %collective-permute-done.5), channel_id=1, source_target_pairs={{1,0},{2,1},{3,2},{4,3},{5,4},{6,5},{7,6},{0,7},{9,8},{10,9},{11,1... | collective-permute-start | bytes 3145736 | tf_op jit(solution)/shard_map/ppermute | solution.py:27
  71.1 3.5 copy-start.6
  222.1 1.4 copy-start.1
  225.2 1.3 copy-start.7
  240.4 6.0 %copy-start.3 = (bf16[16,128,512]{2,1,0:T(8,128)(2,1)S(1)}, bf16[16,128,512]{2,1,0:T(8,128)(2,1)}, u32[]{:S(2)}) copy-start(bf16[16,128,512]{2,1,0:T(8,128)(2,1)} %get-tuple-element.9) | copy-start | bytes 6291460
  240.4 102.4 %all-to-all-start.1 = ((bf16[32,1,128,512]{3,2,1,0:T(8,128)(2,1)}), bf16[32,1,128,512]{3,2,1,0:T(8,128)(2,1)}, u32[]{:S(2)}, u32[]{:S(2)}) async-start(bf16[32,1,128,512]{3,2,1,0:T(8,128)(2,1)} %bitcast.100), calls=%async_computation.1 | async-start | bytes 8388608 | tf_op jit(solution)/shard_map/all_to_all | solution.py:134
  248.5 3.1 copy-start.4
  248.5 3.5 copy-start.8
  253.0 1.0 copy-start.5
  342.8 5.8 %copy-start.2 = (bf16[8,256,4,128]{3,2,1,0:T(4,128)(2,1)S(1)}, bf16[8,256,4,128]{3,2,1,0:T(4,128)(2,1)}, u32[]{:S(2)}) copy-start(bf16[8,256,4,128]{3,2,1,0:T(4,128)(2,1)} %copy-done.1) | copy-start | bytes 6291460
  342.8 102.2 %all-to-all-start = ((bf16[32,1,128,512]{3,2,1,0:T(8,128)(2,1)}), bf16[32,1,128,512]{3,2,1,0:T(8,128)(2,1)}, u32[]{:S(2)}, u32[]{:S(2)}) async-start(bf16[32,1,128,512]{3,2,1,0:T(8,128)(2,1)} %bitcast.99), calls=%async_computation | async-start | bytes 8388608 | tf_op jit(solution)/shard_map/all_to_all | solution.py:133
  445.0 4.7 %copy-start = (bf16[4,8,128,512]{3,1,2,0:T(8,128)(2,1)S(1)}, bf16[4,8,128,512]{3,1,2,0:T(8,128)(2,1)}, u32[]{:S(2)}) copy-start(bf16[4,8,128,512]{3,1,2,0:T(8,128)(2,1)} %copy.130) | copy-start | bytes 12582916
Sparse Core Ops, SparseCore 0:
  10.6 101.2 all-gather.2
  114.5 95.5 all-gather.4
